TPU v7x, 256 devices: a whole 4x4x8 slice. The times are simulated.
256 devices in a mesh: seq: 16 (over x, y), fsdp: 16 (over z, core).
Axes of the slice: x: 4, y: 4, z: 8, core: 2. Of those that a mesh axis runs over, the one named last changes fastest.
Arguments:
- patches: bfloat16 [16, 8704, 1176], P('fsdp', 'seq'), may hold values from -6 to 6
- send_slot: int32 [16, 272], P('fsdp', 'seq'), may hold values from 0 to 271, as said below
- segments: int32 [16, 272], P('fsdp'), may hold values from 0 to 33, never falling along the last dimension, each value on 1 to 24 neighbouring positions
- stem_weight: bfloat16 [3584, 1176], P('fsdp'), may hold values from -0.1875 to 0.1875
- norm_gain: bfloat16 [3584], P('fsdp'), may hold values from 0.099609375 to 1.8984375
- conv_kernel: bfloat16 [5, 3584], P(None, 'fsdp'), may hold values from -3 to 3
- cotangent: bfloat16 [16, 8704, 3584], P('fsdp', 'seq'), may hold values from -6 to 6
Outputs:
- features: bfloat16 [16, 8704, 3584], P('fsdp', 'seq')
- grad_patches: bfloat16 [16, 8704, 1176], P('fsdp', 'seq')
- grad_weight: bfloat16 [3584, 1176], P('fsdp')
- grad_channels: float32 [6, 3584], P(None, 'fsdp')
Inputs may be any that keep to these rules, and one draw needn't show every extreme that they name: `send_slot`: each row is a permutation of the packed slots. At most 2 frame slots of one device go to one device's packed slots, and every device sends exactly 2 to some device; within a row the number that device s sends to device (s + o) modulo the seq axis size depends on o alone. `segments`: ids never fall along a row; a clip holds 1 to 24 slots, one exactly 24.
All inputs are finite; a program needn't handle non-finite values.
Results may differ from a plain program's by a relative error of at most 0.0056.
Values may be sent and summed in bfloat16 or wider, within the bound.
A program may use at most 192 MiB of HBM per device.

v0:
```python
import math
import jax
import jax.numpy as jnp
from jax import lax
from jax.sharding import PartitionSpec as P

EPSILON = 1e-06


def extended_2(cells, sides, width):
    for axis, dim in sides:
        count = lax.axis_size(axis)
        ends = count - 1
        head = lax.slice_in_dim(cells, 0, width, axis=dim)
        tail = lax.slice_in_dim(cells, cells.shape[dim] - width, cells.shape[dim], axis=dim)
        cells = jnp.concatenate(
            [
                lax.ppermute(tail, axis, [(i, (i + 1) % count) for i in range(ends)]),
                cells,
                lax.ppermute(head, axis, [((i + 1) % count, i) for i in range(ends)]),
            ],
            axis=dim,
        )
    return cells


def slot_mask(segment_row, centre):
    slot_total = segment_row.shape[0]
    safe_centre = jnp.clip(centre, 0, slot_total - 1)
    columns = []
    for offset in range(5):
        neighbour = centre + (offset - 2)
        inside = (neighbour >= 0) & (neighbour < slot_total) & (centre >= 0) & (centre < slot_total)
        same_clip = segment_row[jnp.clip(neighbour, 0, slot_total - 1)] == segment_row[safe_centre]
        columns.append((inside & same_clip).astype(jnp.float32))
    return jnp.stack(columns, axis=1)


def temporal_mix(padded, clip_mask, kernel, slot_total):
    kernel_wide = kernel.astype(jnp.float32)
    result = padded[0:slot_total].astype(jnp.float32) * (
        clip_mask[:, 0][:, None, None] * kernel_wide[0][None, None, :]
    )
    for offset in range(1, 5):
        addend = padded[offset : offset + slot_total].astype(jnp.float32) * (
            clip_mask[:, offset][:, None, None] * kernel_wide[offset][None, None, :]
        )
        result = result + addend
    return result


def temporal_back(slope_padded, mask_padded, kernel, slot_total):
    kernel_wide = kernel.astype(jnp.float32)
    result = jnp.zeros((slot_total,) + slope_padded.shape[1:], jnp.float32)
    for offset in range(5):
        first_row = 4 - offset
        weights_row = (
            mask_padded[first_row : first_row + slot_total, offset][:, None, None]
            * kernel_wide[offset][None, None, :]
        )
        result = (
            result
            + slope_padded[first_row : first_row + slot_total].astype(jnp.float32) * weights_row
        )
    return result


def kernel_sums(slope_blocks, padded, clip_mask, slot_total):
    stacked = []
    for offset in range(5):
        product = jnp.sum(
            slope_blocks.astype(jnp.float32)
            * padded[offset : offset + slot_total].astype(jnp.float32),
            axis=1,
        )
        stacked.append(jnp.sum(product * clip_mask[:, offset][:, None], axis=0))
    return jnp.stack(stacked, axis=0)


def rim_rows(values, margin):
    return extended_2(values, (("seq", 0),), margin)


def shards(patches, send_slot, segments, stem_weight, norm_gain, conv_kernel, cotangent):
    seq_size = lax.axis_size("seq")
    fsdp_size = lax.axis_size("fsdp")
    seq_index = lax.axis_index("seq")
    slot_count = send_slot.shape[1]
    tokens = patches.shape[1]
    slot_rows = tokens // slot_count
    pixel_width = patches.shape[2]
    capacity = 2 * slot_count // seq_size
    destination = send_slot[0]
    owner_index = destination // slot_count
    same_owner = owner_index[:, None] == owner_index[None, :]
    earlier = destination[None, :] < destination[:, None]
    ranking = jnp.sum((same_owner & earlier).astype(jnp.int32), axis=1)
    buffer_row = owner_index * capacity + ranking
    frames = patches[0].reshape(slot_count, slot_rows, pixel_width)
    outbox = (
        jnp.zeros((seq_size * capacity, slot_rows, pixel_width), jnp.bfloat16)
        .at[buffer_row]
        .set(frames)
    )
    position = (
        jnp.full((seq_size * capacity,), -1.0, jnp.float32)
        .at[buffer_row]
        .set((destination % slot_count).astype(jnp.float32))
        .astype(jnp.bfloat16)
    )
    incoming, arrived = (
        lax.all_to_all(outbox, "seq", split_axis=0, concat_axis=0, tiled=True),
        lax.all_to_all(position, "seq", split_axis=0, concat_axis=0, tiled=True),
    )
    arrived_float = arrived.astype(jnp.float32)
    target = jnp.where(arrived_float >= 0.0, arrived_float, float(slot_count)).astype(jnp.int32)
    packed = (
        jnp.zeros((slot_count + 1, slot_rows, pixel_width), jnp.bfloat16)
        .at[target]
        .set(incoming)[:slot_count]
        .reshape(tokens, pixel_width)
    )
    weight_full, gain_low, kernel_full = (
        lax.all_gather(stem_weight, "fsdp", axis=0, tiled=True),
        lax.all_gather(norm_gain, "fsdp", axis=0, tiled=True),
        lax.all_gather(conv_kernel, "fsdp", axis=1, tiled=True),
    )
    gain_wide = gain_low.astype(jnp.float32)
    channels = weight_full.shape[0]
    stem_out = lax.dot_general(
        packed, weight_full, (((1,), (1,)), ((), ())), preferred_element_type=jnp.float32
    )
    inv_rms = lax.rsqrt(jnp.mean(stem_out * stem_out, axis=1, keepdims=True) + EPSILON)
    unit_rows = stem_out * inv_rms
    normed = (unit_rows * gain_wide).astype(jnp.bfloat16)
    segment_row = segments[0]
    centre = seq_index * slot_count + jnp.arange(slot_count, dtype=jnp.int32)
    extended = seq_index * slot_count + jnp.arange(-2, slot_count + 2, dtype=jnp.int32)
    clip_mask = slot_mask(segment_row, centre)
    mask_padded = slot_mask(segment_row, extended)
    padded = rim_rows(normed, 2 * slot_rows).reshape(slot_count + 4, slot_rows, channels)
    mixed_rows = temporal_mix(padded, clip_mask, kernel_full, slot_count).reshape(tokens, channels)
    features = (stem_out + jax.nn.silu(mixed_rows)).astype(jnp.bfloat16)
    upstream_wide = cotangent[0].astype(jnp.float32)
    gate_value = jax.nn.sigmoid(mixed_rows)
    slope_low = (upstream_wide * gate_value * (1.0 + mixed_rows * (1.0 - gate_value))).astype(
        jnp.bfloat16
    )
    slope_padded = rim_rows(slope_low, 2 * slot_rows).reshape(slot_count + 4, slot_rows, channels)
    d_normed = temporal_back(slope_padded, mask_padded, kernel_full, slot_count).reshape(
        tokens, channels
    )
    gated = d_normed * gain_wide
    d_stem = upstream_wide + inv_rms * (
        gated - unit_rows * jnp.mean(gated * unit_rows, axis=1, keepdims=True)
    )
    d_stem_low = d_stem.astype(jnp.bfloat16)
    grad_rows = jnp.dot(d_stem_low, weight_full, preferred_element_type=jnp.float32).astype(
        jnp.bfloat16
    )
    gain_part = jnp.sum(d_normed * unit_rows, axis=0)
    slope_blocks = slope_padded[2 : 2 + slot_count]
    kernel_part = kernel_sums(slope_blocks, padded, clip_mask, slot_count)
    chan_terms = jnp.concatenate([gain_part[None, :], kernel_part], axis=0).T
    weight_block = lax.dot_general(
        d_stem_low, packed, (((0,), (0,)), ((), ())), preferred_element_type=jnp.float32
    )
    grad_shard = lax.psum_scatter(
        jnp.concatenate([weight_block, chan_terms], axis=1), "fsdp", scatter_dimension=0, tiled=True
    )
    summed = lax.psum(grad_shard, "seq")
    grad_scale = 1.0 / math.sqrt(tokens * seq_size * fsdp_size)
    grad_weight = (summed[:, :pixel_width] * grad_scale).astype(jnp.bfloat16)
    grad_channels = (summed[:, pixel_width:] * grad_scale).T
    return (features[None], grad_rows[None], grad_weight, grad_channels)


def solution(mesh):
    in_specs = (
        P("fsdp", "seq", None),
        P("fsdp", "seq"),
        P("fsdp", None),
        P("fsdp", None),
        P("fsdp"),
        P(None, "fsdp"),
        P("fsdp", "seq", None),
    )
    out_specs = (P("fsdp", "seq", None), P("fsdp", "seq", None), P("fsdp", None), P(None, "fsdp"))
    return jax.shard_map(shards, mesh=mesh, in_specs=in_specs, out_specs=out_specs, check_vma=False)
```

profile of v0, /device:TPU:32, one launch (start us, length us, event | category | flops | bytes accessed | tf_op | source)
XLA Modules:
  0.0 471.1 jit_solution(15271871692152045158)
XLA Ops:
  9.3 0.9 convert_reduce_fusion
  12.2 7.0 %all-to-all-start = ((bf16[16,2,1]{1,2,0:T(2,128)(2,1)}), bf16[16,2,1]{1,2,0:T(2,128)(2,1)S(1)}, u32[]{:S(2)}, u32[]{:S(2)}) async-start(bf16[16,2,1]{1,2,0:T(2,128)(2,1)} %all_to_all.12), calls=%async_computation | async-start | bytes 16384 | tf_op jit(solution)/shard_map/all_to_all | solution.py:113
  19.3 0.7 gather_fusion.5
  20.0 0.7 gather_fusion.6
  20.8 0.7 gather_fusion.8
  21.5 0.7 gather_fusion.7
  23.0 18.3 %all-gather = bf16[16,224,5]{1,2,0:T(8,128)(2,1)S(1)} all-gather(bf16[1,224,5]{1,2,0:T(8,128)(2,1)} %bitcast.126), channel_id=1, replica_groups=mesh['seq'=16,'fsdp'=16] {'fsdp'}, dimensions={0}, use_global_device_ids=true | all-gather | bytes 38080 | tf_op jit(solution)/shard_map/all_gather | solution.py:126
  45.6 0.8 broadcast_multiply_fusion
  46.4 0.9 broadcast_multiply_fusion.1
  47.4 1.8 broadcast_in_dim.19
  49.2 5.8 %scatter_fusion = bf16[32,32,1176]{2,1,0:T(8,128)(2,1)} fusion(bf16[32,32,1176]{2,1,0:T(8,128)(2,1)} %broadcast_in_dim.19, s32[17]{0:T(128)S(1)} %fusion.26, bf16[17,32,1176]{2,1,0:T(8,128)(2,1)S(1)} %bitcast.120), kind=kCustom, calls=%fused_computation.11 | custom fusion | bytes 3838532 | tf_op jit(solution)/shard_map/scatter | solution.py:103
  55.0 7.3 %all-to-all-start.1 = ((bf16[32,32,1176]{2,1,0:T(8,128)(2,1)}), bf16[32,32,1176]{2,1,0:T(8,128)(2,1)}, u32[]{:S(2)}, u32[]{:S(2)}) async-start(bf16[32,32,1176]{2,1,0:T(8,128)(2,1)} %scatter_fusion), calls=%async_computation.1 | async-start | bytes 5242880 | tf_op jit(solution)/shard_map/all_to_all | solution.py:112
  63.9 24.1 %all-reduce = bf16[3584]{0:T(1024)(128)(2,1)S(1)} all-reduce(bf16[3584]{0:T(1024)(128)(2,1)S(1)} %dynamic-update-slice), channel_id=1, replica_groups=mesh['seq'=16,'fsdp'=16] {'fsdp'}, use_global_device_ids=true, to_apply=%add | all-reduce | flops 3584 | bytes 14336
  88.1 1.0 broadcast_multiply_fusion.2
  89.0 1.0 broadcast_multiply_fusion.3
  90.1 8.8 %all-to-all-done.1 = bf16[32,32,1176]{2,1,0:T(8,128)(2,1)} async-done(((bf16[32,32,1176]{2,1,0:T(8,128)(2,1)}), bf16[32,32,1176]{2,1,0:T(8,128)(2,1)}, u32[]{:S(2)}, u32[]{:S(2)}) %all-to-all-start.1) | async-done | bytes 2408480 | tf_op jit(solution)/shard_map/all_to_all | solution.py:112
  99.1 4.2 scatter_fusion.1
  103.4 8.0 %multiply_reduce_fusion.2 = (f32[544]{0:T(1024)S(1)}, f32[544,3584]{1,0:T(8,128)S(1)}) fusion(bf16[544,1176]{1,0:T(8,128)(2,1)S(1)} %bitcast.121, bf16[3584,1176]{1,0:T(8,128)(2,1)} %all-gather.3.cloned.1.call-done), kind=kOutput, calls=%fused_computation.47 | convolution fusion | flops 4589583872 | bytes 17510016 | tf_op jit(solution)/shard_map/dot_general | solution.py:130
  111.5 1.3 multiply_convert_fusion
  112.9 1.6 collective-permute-start.1
  114.5 4.8 %collective-permute-start = (bf16[64,3584]{1,0:T(8,128)(2,1)S(1)}, bf16[64,3584]{1,0:T(8,128)(2,1)S(1)}, u32[]{:S(2)}, u32[]{:S(2)}) collective-permute-start(bf16[64,3584]{1,0:T(8,128)(2,1)S(1)} %get-tuple-element.46), channel_id=1, source_target_pairs={{0,16},{16,32},{32,48},{48,64},{64,80},{80,96},{96,112},{112,128},... | collective-permute-start | bytes 1376264 | tf_op jit(solution)/shard_map/ppermute | solution.py:18
  119.3 0.9 broadcast_multiply_fusion.4
  120.2 5.8 %collective-permute-done.1 = bf16[64,3584]{1,0:T(8,128)(2,1)S(1)} collective-permute-done((bf16[64,3584]{1,0:T(8,128)(2,1)S(1)}, bf16[64,3584]{1,0:T(8,128)(2,1)S(1)}, u32[]{:S(2)}, u32[]{:S(2)}) %collective-permute-start.1) | collective-permute-done | bytes 458784 | tf_op jit(solution)/shard_map/ppermute | solution.py:20
  126.0 1.3 collective-permute-done
  127.4 8.3 %convert_multiply_fusion = (f32[544,3584]{1,0:T(8,128)}, bf16[544,3584]{1,0:T(8,128)(2,1)S(1)}, f32[544,3584]{1,0:T(8,128)}) fusion(bf16[64,3584]{1,0:T(8,128)(2,1)S(1)} %collective-permute-done.1, bf16[544,3584]{1,0:T(8,128)(2,1)S(1)} %multiply_convert_fusion, bf16[1,544,3584]{2,1,0:T(8,128)(2,1)S(1)} %copy-done.5, f32[17,3584]{1,0:T(8,128)S(1)} %copy-done.7, ...), kind=kLoop, calls=%fused_computation.13 | loop fusion | flops 74088448 | bytes 29431808 | tf_op jit(solution)/shard_map/mul | solution.py:72
  135.7 1.9 copy-done.3
  137.6 0.8 fusion.45
  138.4 5.5 %collective-permute-start.3 = (bf16[64,3584]{1,0:T(8,128)(2,1)}, bf16[64,3584]{1,0:T(8,128)(2,1)}, u32[]{:S(2)}, u32[]{:S(2)}) collective-permute-start(bf16[64,3584]{1,0:T(8,128)(2,1)} %get-tuple-element.45), channel_id=1, source_target_pairs={{0,16},{16,32},{32,48},{48,64},{64,80},{80,96},{96,112},{112,128},... | collective-permute-start | bytes 1376264 | tf_op jit(solution)/shard_map/ppermute | solution.py:18
  143.9 1.5 collective-permute-start.2
  145.4 15.1 %convert_multiply_fusion.1 = (f32[544,3584]{1,0:T(8,128)}, f32[544,3584]{1,0:T(8,128)}, f32[544,3584]{1,0:T(8,128)}, f32[544,3584]{1,0:T(8,128)}) fusion(bf16[544,3584]{1,0:T(8,128)(2,1)} %copy-done.3, bf16[64,3584]{1,0:T(8,128)(2,1)S(1)} %collective-permute-done.1, bf16[544,3584]{1,0:T(8,128)(2,1)} %copy-done.4, bf16[64,3584]{1,0:T(8,128)(2,1)S(1)} %collective-permute-done), kind=kLoop, calls=%fused_computation.14 | loop fusion | flops 35094528 | bytes 39911424 | tf_op jit(solution)/shard_map/mul | solution.py:72
  160.5 4.3 reduce_sum.133
  165.0 4.4 reduce_sum.135
  169.5 4.4 reduce_sum.137
  174.0 4.4 reduce_sum.139
  178.5 4.4 reduce_sum.141
  183.0 10.2 %fusion.9 = f32[544,3584]{1,0:T(8,128)S(1)} fusion(bf16[544,3584]{1,0:T(8,128)(2,1)} %copy-done.3, bf16[64,3584]{1,0:T(8,128)(2,1)} %collective-permute-done.3, bf16[64,3584]{1,0:T(8,128)(2,1)} %collective-permute-done.2, f32[17,3584]{1,0:T(8,128)S(1)} %get-tuple-element.56, f32[17,3584]{1,0:T(8,128)} %get-tuple-element.54, ...), kind=kLoop, calls=%fused_computation.36 | loop fusion | flops 50692096 | bytes 13834240 | tf_op jit(solution)/shard_map/add | solution.py:62
  193.3 2.1 multiply_reduce_fusion
  195.4 9.9 %fusion.6 = (bf16[544,3584]{1,0:T(8,128)(2,1)}, bf16[1,544,3584]{2,1,0:T(8,128)(2,1)}) fusion(f32[544,3584]{1,0:T(8,128)S(1)} %fusion.9, f32[544,3584]{1,0:T(8,128)S(1)} %bitcast.114, bf16[1,544,3584]{2,1,0:T(8,128)(2,1)} %param.13, f32[544]{0:T(1024)S(1)} %broadcast_multiply_fusion.10, f32[3584]{0:T(1024)S(1)} %convert_element_type.185, ...), kind=kLoop, calls=%fused_computation.33 | loop fusion | flops 27295744 | bytes 35113216 | tf_op jit(solution)/shard_map/convert_element_type | solution.py:157
  205.3 12.7 %fusion.47 = f32[3584,1176]{0,1:T(8,128)} fusion(bf16[544,3584]{1,0:T(8,128)(2,1)} %get-tuple-element.42, bf16[544,1176]{1,0:T(8,128)(2,1)S(1)} %bitcast.122), kind=kOutput, calls=%fused_computation.172 | convolution fusion | flops 4585684992 | bytes 22038016 | tf_op jit(solution)/shard_map/dot_general | solution.py:165
  218.1 11.5 %pad_maximum_fusion = f32[3584,1182]{0,1:T(8,128)} fusion(f32[3584,6]{0,1:T(8,128)S(1)} %bitcast.123, f32[3584,1176]{0,1:T(8,128)} %fusion.47), kind=kLoop, calls=%fused_computation.19 | loop fusion | flops 4236288 | bytes 33890304 | tf_op jit(solution)/shard_map/concatenate | solution.py:169
  229.6 18.8 %copy.23 = f32[3584,1182]{1,0:T(8,128)} copy(f32[3584,1182]{0,1:T(8,128)} %pad_maximum_fusion) | data formatting | bytes 33890304
  248.5 109.9 %reduce-scatter.4.cloned.1.call-done = f32[224,1182]{1,0:T(8,128)} async-done(((f32[3584,1182]{1,0:T(8,128)}), f32[224,1182]{1,0:T(8,128)}) %reduce-scatter.4.cloned.1.call-update) | async-done | bytes 1059088
  358.4 2.7 copy.24
  361.1 10.4 %fusion.16 = bf16[1,544,1176]{2,1,0:T(8,128)(2,1)} fusion(bf16[544,3584]{1,0:T(8,128)(2,1)} %get-tuple-element.42, bf16[3584,1176]{1,0:T(8,128)(2,1)} %all-gather.3.cloned.1.call-done), kind=kOutput, calls=%fused_computation.66 | convolution fusion | flops 4586324992 | bytes 13608448 | tf_op jit(solution)/shard_map/dot_general | solution.py:158
  371.5 89.3 %all-reduce.3.cloned.1.call-done = f32[224,1182]{0,1:T(8,128)} async-done(((f32[224,1182]{0,1:T(8,128)}), f32[224,1182]{0,1:T(8,128)}) %all-reduce.3.cloned.1.call-update) | async-done | bytes 1059088 | tf_op jit(solution)/shard_map/psum | solution.py:171
  460.8 1.4 fusion.17
  462.2 1.0 copy.22
  463.3 1.3 fusion.18
  (107 shorter events, 11.4 us)
Async XLA Ops:
  7.2 12.1 %copy-start = (s32[1,272]{1,0:T(1,128)S(1)}, s32[1,272]{1,0:T(1,128)}, u32[]{:S(2)}) copy-start(s32[1,272]{1,0:T(1,128)} %param.9) | copy-start | bytes 3268
  7.2 42.0 %copy-start.6 = (bf16[1,544,1176]{2,1,0:T(8,128)(2,1)S(1)}, bf16[1,544,1176]{2,1,0:T(8,128)(2,1)}, u32[]{:S(2)}) copy-start(bf16[1,544,1176]{2,1,0:T(8,128)(2,1)} %param.7) | copy-start | bytes 3838468
  7.2 96.2 %all-gather.3.cloned.1.call-start = ((), (), s32[]{:S(2)}) async-start(), calls=%async_computation.3 | async-start | bytes 9748480 | tf_op jit(solution)/shard_map/all_gather | solution.py:124
  12.2 42.8 %all-to-all-start = ((bf16[16,2,1]{1,2,0:T(2,128)(2,1)}), bf16[16,2,1]{1,2,0:T(2,128)(2,1)S(1)}, u32[]{:S(2)}, u32[]{:S(2)}) async-start(bf16[16,2,1]{1,2,0:T(2,128)(2,1)} %all_to_all.12), calls=%async_computation | async-start | bytes 16384 | tf_op jit(solution)/shard_map/all_to_all | solution.py:113
  42.2 20.2 %copy-start.12 = (u32[256]{0:T(256)S(1)}, u32[256]{0:T(256)}, u32[]{:S(2)}) copy-start(u32[256]{0:T(256)} %constant.79) | copy-start | bytes 3076
  42.2 21.5 %copy-start.11 = (bf16[224]{0:T(256)(128)(2,1)S(1)}, bf16[224]{0:T(256)(128)(2,1)}, u32[]{:S(2)}) copy-start(bf16[224]{0:T(256)(128)(2,1)} %param.11) | copy-start | bytes 1348
  55.0 43.9 %all-to-all-start.1 = ((bf16[32,32,1176]{2,1,0:T(8,128)(2,1)}), bf16[32,32,1176]{2,1,0:T(8,128)(2,1)}, u32[]{:S(2)}, u32[]{:S(2)}) async-start(bf16[32,32,1176]{2,1,0:T(8,128)(2,1)} %scatter_fusion), calls=%async_computation.1 | async-start | bytes 5242880 | tf_op jit(solution)/shard_map/all_to_all | solution.py:112
  62.3 296.1 %reduce-scatter.4.cloned.1.call-start = ((), (), s32[]{:S(2)}) async-start(), calls=%async_computation.5 | async-start | bytes 19496960
  111.4 24.2 %copy-start.2 = (f32[544,3584]{1,0:T(8,128)}, f32[544,3584]{1,0:T(8,128)S(1)}, u32[]{:S(2)}) copy-start(f32[544,3584]{1,0:T(8,128)S(1)} %get-tuple-element.69) | copy-start | bytes 23396356
  111.4 15.9 %copy-start.5 = (bf16[1,544,3584]{2,1,0:T(8,128)(2,1)S(1)}, bf16[1,544,3584]{2,1,0:T(8,128)(2,1)}, u32[]{:S(2)}) copy-start(bf16[1,544,3584]{2,1,0:T(8,128)(2,1)} %param.13) | copy-start | bytes 11698180
  111.5 15.9 %copy-start.7 = (f32[17,3584]{1,0:T(8,128)S(1)}, f32[17,3584]{1,0:T(8,128)}, u32[]{:S(2)}) copy-start(f32[17,3584]{1,0:T(8,128)} %get-tuple-element.57) | copy-start | bytes 731140
  111.5 15.9 %copy-start.8 = (f32[17,3584]{1,0:T(8,128)S(1)}, f32[17,3584]{1,0:T(8,128)}, u32[]{:S(2)}) copy-start(f32[17,3584]{1,0:T(8,128)} %get-tuple-element.55) | copy-start | bytes 731140
  111.5 15.9 %copy-start.9 = (f32[17,3584]{1,0:T(8,128)S(1)}, f32[17,3584]{1,0:T(8,128)}, u32[]{:S(2)}) copy-start(f32[17,3584]{1,0:T(8,128)} %get-tuple-element.53) | copy-start | bytes 731140
  111.5 15.9 %copy-start.10 = (f32[17,3584]{1,0:T(8,128)S(1)}, f32[17,3584]{1,0:T(8,128)}, u32[]{:S(2)}) copy-start(f32[17,3584]{1,0:T(8,128)} %get-tuple-element.51) | copy-start | bytes 731140
  112.8 22.9 %copy-start.4 = (bf16[544,3584]{1,0:T(8,128)(2,1)}, bf16[544,3584]{1,0:T(8,128)(2,1)S(1)}, u32[]{:S(2)}) copy-start(bf16[544,3584]{1,0:T(8,128)(2,1)S(1)} %multiply_convert_fusion) | copy-start | bytes 11698180
  112.9 13.1 %collective-permute-start.1 = (bf16[64,3584]{1,0:T(8,128)(2,1)S(1)}, bf16[64,3584]{1,0:T(8,128)(2,1)S(1)}, u32[]{:S(2)}, u32[]{:S(2)}) collective-permute-start(bf16[64,3584]{1,0:T(8,128)(2,1)S(1)} %get-tuple-element.47), channel_id=1, source_target_pairs={{16,0},{32,16},{48,32},{64,48},{80,64},{96,80},{112,96},{128,112},... | collective-permute-start | bytes 1376264 | tf_op jit(solution)/shard_map/ppermute | solution.py:20
  114.5 12.9 %collective-permute-start = (bf16[64,3584]{1,0:T(8,128)(2,1)S(1)}, bf16[64,3584]{1,0:T(8,128)(2,1)S(1)}, u32[]{:S(2)}, u32[]{:S(2)}) collective-permute-start(bf16[64,3584]{1,0:T(8,128)(2,1)S(1)} %get-tuple-element.46), channel_id=1, source_target_pairs={{0,16},{16,32},{32,48},{48,64},{64,80},{80,96},{96,112},{112,128},... | collective-permute-start | bytes 1376264 | tf_op jit(solution)/shard_map/ppermute | solution.py:18
  135.7 1.9 copy-start.3
  138.4 44.6 %collective-permute-start.3 = (bf16[64,3584]{1,0:T(8,128)(2,1)}, bf16[64,3584]{1,0:T(8,128)(2,1)}, u32[]{:S(2)}, u32[]{:S(2)}) collective-permute-start(bf16[64,3584]{1,0:T(8,128)(2,1)} %get-tuple-element.45), channel_id=1, source_target_pairs={{0,16},{16,32},{32,48},{48,64},{64,80},{80,96},{96,112},{112,128},... | collective-permute-start | bytes 1376264 | tf_op jit(solution)/shard_map/ppermute | solution.py:18
  143.9 39.1 %collective-permute-start.2 = (bf16[64,3584]{1,0:T(8,128)(2,1)S(1)}, bf16[64,3584]{1,0:T(8,128)(2,1)}, u32[]{:S(2)}, u32[]{:S(2)}) collective-permute-start(bf16[64,3584]{1,0:T(8,128)(2,1)S(1)} %get-tuple-element.44), channel_id=1, source_target_pairs={{16,0},{32,16},{48,32},{64,48},{80,64},{96,80},{112,96},{128,112},... | collective-permute-start | bytes 1376264 | tf_op jit(solution)/shard_map/ppermute | solution.py:20
  182.8 10.4 %slice-start = ((s8[7798784]{0:T(1024)(128)(4,1)}), s8[4194304]{0:T(1024)(128)(4,1)S(1)}, s32[]{:S(2)}) async-start(s8[7798784]{0:T(1024)(128)(4,1)} %bitcast.113), calls=%async_computation.6 | async-start | bytes 8388608
  183.0 10.3 %slice-start.1 = ((s8[7798784]{0:T(1024)(128)(4,1)}), s8[3604480]{0:T(1024)(128)(4,1)S(1)}, s32[]{:S(2)}) async-start(s8[7798784]{0:T(1024)(128)(4,1)} %bitcast.113), calls=%async_computation.7 | async-start | bytes 7208960
  248.5 212.3 %all-reduce.3.cloned.1.call-start = ((), (), s32[]{:S(2)}) async-start(), calls=%async_computation.4 | async-start | bytes 2424832 | tf_op jit(solution)/shard_map/psum | solution.py:171
  361.1 103.5 %copy-start.1 = (s32[1,272]{1,0:T(1,128)S(1)}, s32[1,272]{1,0:T(1,128)}, u32[]{:S(2)}) copy-start(s32[1,272]{1,0:T(1,128)} %param.9) | copy-start | bytes 3268
Sparse Core Ops, SparseCore 0:
  9.9 60.7 all-gather.2
  248.6 109.7 reduce-scatter.3
  361.7 99.0 all-reduce.2
where the time goes:
time: 472 us; the launch traced here: 471 us
  waiting for transfers between devices  216 us (46%)
  other arithmetic  91.6 us (19%)
  local copies, waits for them, and re-layouts  47.3 us (10%)
  blocking collectives  42.4 us (9%)
  matrix products  31.1 us (7%)
  starting transfers between devices  27.8 us (6%)
  between operations  15 us (3%)
    unnamed x4, waiting for transfers between devices  111 us
    psum x1, waiting for transfers between devices, shards(): summed = lax.psum(grad_shard, 'seq')  89.3 us
    unnamed x36, local copies, waits for them, and re-layouts  25.4 us
    unnamed x1, blocking collectives  24.1 us
    mul x2, other arithmetic, kernel_sums(): slope_blocks.astype(jnp.float32)  23.4 us
    reduce_sum x5, other arithmetic, kernel_sums(): jnp.sum(slope_blocks.astype(jnp.float32) * padded[offset:offset + slot_to...  21.8 us
    all_gather x1, blocking collectives, shards(): lax.all_gather(conv_kernel, 'fsdp', axis=1, tiled=True)  18.3 us
    dot_general x1, matrix products, shards(): lax.dot_general(d_stem_low, packed, (((0,), (0,)), ((), ())), preferred_e...  12.7 us
  transfers between devices with their start and end apart: 9, of which 5 were waited for; matrix products, arithmetic and copies ran while one was open for 16% of the time, Pallas kernels for 0%

commit v1 on v0

--- a/solution.py
+++ b/solution.py
@@ -168,7 +168,7 @@
     grad_shard = lax.psum_scatter(
         jnp.concatenate([weight_block, chan_terms], axis=1), "fsdp", scatter_dimension=0, tiled=True
     )
-    summed = lax.psum(grad_shard, "seq")
+    summed = jnp.sum(lax.all_gather(grad_shard, "seq"), axis=0)
     grad_scale = 1.0 / math.sqrt(tokens * seq_size * fsdp_size)
     grad_weight = (summed[:, :pixel_width] * grad_scale).astype(jnp.bfloat16)
     grad_channels = (summed[:, pixel_width:] * grad_scale).T

time: 472 us -> 505 us (1.070)
  waiting for transfers between devices: 216 us -> 245 us
  other arithmetic: 91.6 us -> 97.3 us
    all_gather x0 -> x1, waiting for transfers between devices: none -> 118 us  [shards(): summed = jnp.sum(lax.all_gather(grad_shard, 'seq'), axis=0)]
    unnamed x4 -> x3, waiting for transfers between devices: 111 us -> 0.71 us
    reduce_scatter x0 -> x1, waiting for transfers between devices: none -> 110 us  [shards(): lax.psum_scatter(jnp.concatenate([weight_block, chan_terms], axis=1), 'fs...]
    psum x1 -> x0, waiting for transfers between devices: 89.3 us -> none  [shards(): summed = lax.psum(grad_shard, 'seq')]
    reduce_sum x0 -> x1, other arithmetic: none -> 7.47 us  [shards(): summed = jnp.sum(lax.all_gather(grad_shard, 'seq'), axis=0)]
    unnamed x36 -> x35, local copies, waits for them, and re-layouts: 25.4 us -> 22.3 us
  transfers between devices with their start and end apart: 9 -> 9, of which waited for: 5 -> 5; matrix products, arithmetic and copies ran while one was open for 16% -> 15% of each run, Pallas kernels for 0% -> 0%
where the time goes in v1:
time: 505 us; the launch traced here: 502 us
  waiting for transfers between devices  245 us (49%)
  other arithmetic  97.3 us (19%)
  local copies, waits for them, and re-layouts  44.2 us (9%)
  blocking collectives  42.4 us (8%)
  matrix products  31.1 us (6%)
  starting transfers between devices  27.8 us (6%)
  between operations  15 us (3%)
    all_gather x1, waiting for transfers between devices, shards(): summed = jnp.sum(lax.all_gather(grad_shard, 'seq'), axis=0)  118 us
    reduce_scatter x1, waiting for transfers between devices, shards(): lax.psum_scatter(jnp.concatenate([weight_block, chan_terms], axis=1), 'fs...  110 us
    unnamed x1, blocking collectives  24.1 us
    mul x2, other arithmetic, kernel_sums(): slope_blocks.astype(jnp.float32)  23.4 us
    unnamed x35, local copies, waits for them, and re-layouts  22.3 us
    reduce_sum x5, other arithmetic, kernel_sums(): jnp.sum(slope_blocks.astype(jnp.float32) * padded[offset:offset + slot_to...  21.8 us
    all_gather x1, blocking collectives, shards(): lax.all_gather(conv_kernel, 'fsdp', axis=1, tiled=True)  18.3 us
    dot_general x1, matrix products, shards(): lax.dot_general(d_stem_low, packed, (((0,), (0,)), ((), ())), preferred_e...  12.7 us
  transfers between devices with their start and end apart: 9, of which 5 were waited for; matrix products, arithmetic and copies ran while one was open for 15% of the time, Pallas kernels for 0%

profile of v1, /device:TPU:32, one launch (start us, length us, event | category | flops | bytes accessed | tf_op | source)
XLA Modules:
  0.0 502.5 jit_solution(15845633530079855964)
XLA Ops:
  9.3 0.9 convert_reduce_fusion
  12.2 7.0 %all-to-all-start = ((bf16[16,2,1]{1,2,0:T(2,128)(2,1)}), bf16[16,2,1]{1,2,0:T(2,128)(2,1)S(1)}, u32[]{:S(2)}, u32[]{:S(2)}) async-start(bf16[16,2,1]{1,2,0:T(2,128)(2,1)} %all_to_all.12), calls=%async_computation | async-start | bytes 16384 | tf_op jit(solution)/shard_map/all_to_all | solution.py:113
  19.3 0.7 gather_fusion.5
  20.0 0.7 gather_fusion.6
  20.8 0.7 gather_fusion.8
  21.5 0.7 gather_fusion.7
  23.0 18.3 %all-gather.1 = bf16[16,224,5]{1,2,0:T(8,128)(2,1)S(1)} all-gather(bf16[1,224,5]{1,2,0:T(8,128)(2,1)} %bitcast.128), channel_id=1, replica_groups=mesh['seq'=16,'fsdp'=16] {'fsdp'}, dimensions={0}, use_global_device_ids=true | all-gather | bytes 38080 | tf_op jit(solution)/shard_map/all_gather | solution.py:126
  42.9 0.7 gather_fusion.3
  43.7 0.7 gather_fusion.2
  45.6 0.8 broadcast_multiply_fusion
  46.4 0.9 broadcast_multiply_fusion.1
  47.4 1.8 broadcast_in_dim.19
  49.2 5.8 %scatter_fusion = bf16[32,32,1176]{2,1,0:T(8,128)(2,1)} fusion(bf16[32,32,1176]{2,1,0:T(8,128)(2,1)} %broadcast_in_dim.19, s32[17]{0:T(128)S(1)} %fusion.26, bf16[17,32,1176]{2,1,0:T(8,128)(2,1)S(1)} %bitcast.122), kind=kCustom, calls=%fused_computation.11 | custom fusion | bytes 3838532 | tf_op jit(solution)/shard_map/scatter | solution.py:103
  55.0 7.3 %all-to-all-start.1 = ((bf16[32,32,1176]{2,1,0:T(8,128)(2,1)}), bf16[32,32,1176]{2,1,0:T(8,128)(2,1)}, u32[]{:S(2)}, u32[]{:S(2)}) async-start(bf16[32,32,1176]{2,1,0:T(8,128)(2,1)} %scatter_fusion), calls=%async_computation.1 | async-start | bytes 5242880 | tf_op jit(solution)/shard_map/all_to_all | solution.py:112
  63.9 24.1 %all-reduce = bf16[3584]{0:T(1024)(128)(2,1)S(1)} all-reduce(bf16[3584]{0:T(1024)(128)(2,1)S(1)} %dynamic-update-slice), channel_id=1, replica_groups=mesh['seq'=16,'fsdp'=16] {'fsdp'}, use_global_device_ids=true, to_apply=%add | all-reduce | flops 3584 | bytes 14336
  88.1 1.0 broadcast_multiply_fusion.2
  89.0 1.0 broadcast_multiply_fusion.3
  90.1 8.8 %all-to-all-done.1 = bf16[32,32,1176]{2,1,0:T(8,128)(2,1)} async-done(((bf16[32,32,1176]{2,1,0:T(8,128)(2,1)}), bf16[32,32,1176]{2,1,0:T(8,128)(2,1)}, u32[]{:S(2)}, u32[]{:S(2)}) %all-to-all-start.1) | async-done | bytes 2408480 | tf_op jit(solution)/shard_map/all_to_all | solution.py:112
  99.1 4.2 scatter_fusion.1
  103.4 8.0 %multiply_reduce_fusion.2 = (f32[544]{0:T(1024)S(1)}, f32[544,3584]{1,0:T(8,128)S(1)}) fusion(bf16[544,1176]{1,0:T(8,128)(2,1)S(1)} %bitcast.123, bf16[3584,1176]{1,0:T(8,128)(2,1)} %all-gather.5.cloned.1.call-done), kind=kOutput, calls=%fused_computation.47 | convolution fusion | flops 4589583872 | bytes 17510016 | tf_op jit(solution)/shard_map/dot_general | solution.py:130
  111.5 1.3 multiply_convert_fusion
  112.9 1.6 collective-permute-start.1
  114.5 4.8 collective-permute-start
  119.3 0.9 broadcast_multiply_fusion.4
  120.2 5.8 %collective-permute-done.1 = bf16[64,3584]{1,0:T(8,128)(2,1)S(1)} collective-permute-done((bf16[64,3584]{1,0:T(8,128)(2,1)S(1)}, bf16[64,3584]{1,0:T(8,128)(2,1)S(1)}, u32[]{:S(2)}, u32[]{:S(2)}) %collective-permute-start.1) | collective-permute-done | bytes 458784 | tf_op jit(solution)/shard_map/ppermute | solution.py:20
  126.0 1.3 collective-permute-done
  127.4 8.3 %convert_multiply_fusion = (f32[544,3584]{1,0:T(8,128)}, bf16[544,3584]{1,0:T(8,128)(2,1)S(1)}, f32[544,3584]{1,0:T(8,128)}) fusion(bf16[64,3584]{1,0:T(8,128)(2,1)S(1)} %collective-permute-done.1, bf16[544,3584]{1,0:T(8,128)(2,1)S(1)} %multiply_convert_fusion, bf16[1,544,3584]{2,1,0:T(8,128)(2,1)S(1)} %copy-done.5, f32[17,3584]{1,0:T(8,128)S(1)} %copy-done.7, ...), kind=kLoop, calls=%fused_computation.13 | loop fusion | flops 74088448 | bytes 29431808 | tf_op jit(solution)/shard_map/mul | solution.py:72
  135.7 1.9 copy-done.3
  137.6 0.8 fusion.45
  138.4 5.5 %collective-permute-start.3 = (bf16[64,3584]{1,0:T(8,128)(2,1)}, bf16[64,3584]{1,0:T(8,128)(2,1)}, u32[]{:S(2)}, u32[]{:S(2)}) collective-permute-start(bf16[64,3584]{1,0:T(8,128)(2,1)} %get-tuple-element.45), channel_id=1, source_target_pairs={{0,16},{16,32},{32,48},{48,64},{64,80},{80,96},{96,112},{112,128},... | collective-permute-start | bytes 1376264 | tf_op jit(solution)/shard_map/ppermute | solution.py:18
  143.9 1.5 collective-permute-start.2
  145.4 15.1 %convert_multiply_fusion.1 = (f32[544,3584]{1,0:T(8,128)}, f32[544,3584]{1,0:T(8,128)}, f32[544,3584]{1,0:T(8,128)}, f32[544,3584]{1,0:T(8,128)}) fusion(bf16[544,3584]{1,0:T(8,128)(2,1)} %copy-done.3, bf16[64,3584]{1,0:T(8,128)(2,1)S(1)} %collective-permute-done.1, bf16[544,3584]{1,0:T(8,128)(2,1)} %copy-done.4, bf16[64,3584]{1,0:T(8,128)(2,1)S(1)} %collective-permute-done), kind=kLoop, calls=%fused_computation.14 | loop fusion | flops 35094528 | bytes 39911424 | tf_op jit(solution)/shard_map/mul | solution.py:72
  160.5 4.3 reduce_sum.142
  165.0 4.4 reduce_sum.144
  169.5 4.4 reduce_sum.146
  174.0 4.4 reduce_sum.148
  178.5 4.4 reduce_sum.150
  183.0 10.2 %fusion.9 = f32[544,3584]{1,0:T(8,128)S(1)} fusion(bf16[544,3584]{1,0:T(8,128)(2,1)} %copy-done.3, bf16[64,3584]{1,0:T(8,128)(2,1)} %collective-permute-done.3, bf16[64,3584]{1,0:T(8,128)(2,1)} %collective-permute-done.2, f32[17,3584]{1,0:T(8,128)S(1)} %get-tuple-element.56, f32[17,3584]{1,0:T(8,128)} %get-tuple-element.54, ...), kind=kLoop, calls=%fused_computation.36 | loop fusion | flops 50692096 | bytes 13834240 | tf_op jit(solution)/shard_map/add | solution.py:62
  193.3 2.1 multiply_reduce_fusion
  195.4 9.9 %fusion.6 = (bf16[544,3584]{1,0:T(8,128)(2,1)}, bf16[1,544,3584]{2,1,0:T(8,128)(2,1)}) fusion(f32[544,3584]{1,0:T(8,128)S(1)} %fusion.9, f32[544,3584]{1,0:T(8,128)S(1)} %bitcast.115, bf16[1,544,3584]{2,1,0:T(8,128)(2,1)} %param.13, f32[544]{0:T(1024)S(1)} %broadcast_multiply_fusion.10, f32[3584]{0:T(1024)S(1)} %convert_element_type.185, ...), kind=kLoop, calls=%fused_computation.33 | loop fusion | flops 27295744 | bytes 35113216 | tf_op jit(solution)/shard_map/convert_element_type | solution.py:157
  205.3 12.7 %fusion.47 = f32[3584,1176]{0,1:T(8,128)} fusion(bf16[544,3584]{1,0:T(8,128)(2,1)} %get-tuple-element.42, bf16[544,1176]{1,0:T(8,128)(2,1)S(1)} %bitcast.124), kind=kOutput, calls=%fused_computation.172 | convolution fusion | flops 4585684992 | bytes 22038016 | tf_op jit(solution)/shard_map/dot_general | solution.py:165
  218.1 11.5 %pad_maximum_fusion = f32[3584,1182]{0,1:T(8,128)} fusion(f32[3584,6]{0,1:T(8,128)S(1)} %bitcast.125, f32[3584,1176]{0,1:T(8,128)} %fusion.47), kind=kLoop, calls=%fused_computation.19 | loop fusion | flops 4236288 | bytes 33890304 | tf_op jit(solution)/shard_map/concatenate | solution.py:169
  229.6 18.8 %copy.27 = f32[3584,1182]{1,0:T(8,128)} copy(f32[3584,1182]{0,1:T(8,128)} %pad_maximum_fusion) | data formatting | bytes 33890304
  248.4 109.8 %reduce-scatter.4.cloned.1.call-done = f32[224,1182]{1,0:T(8,128)} async-done(((f32[3584,1182]{1,0:T(8,128)}), f32[224,1182]{1,0:T(8,128)}) %reduce-scatter.4.cloned.1.call-update) | async-done | bytes 1059088 | tf_op jit(solution)/shard_map/reduce_scatter | solution.py:168
  358.3 10.4 %fusion.16 = bf16[1,544,1176]{2,1,0:T(8,128)(2,1)} fusion(bf16[544,3584]{1,0:T(8,128)(2,1)} %get-tuple-element.42, bf16[3584,1176]{1,0:T(8,128)(2,1)} %all-gather.5.cloned.1.call-done), kind=kOutput, calls=%fused_computation.66 | convolution fusion | flops 4586324992 | bytes 13608448 | tf_op jit(solution)/shard_map/dot_general | solution.py:158
  368.7 118.0 %all-gather.7.cloned.1.call-done = f32[3584,1182]{1,0:T(8,128)} async-done(((f32[224,1182]{1,0:T(8,128)}), f32[3584,1182]{1,0:T(8,128)}) %all-gather.7.cloned.1.call-update) | async-done | bytes 16945168 | tf_op jit(solution)/shard_map/all_gather | solution.py:171
  486.8 7.5 %reduce_sum.152 = f32[224,1182]{1,0:T(8,128)S(1)} reduce(f32[16,224,1182]{2,1,0:T(8,128)} %bitcast.121, f32[]{:T(128)} %constant.28.clone.1), dimensions={0}, to_apply=%region_18.19 | reduce | flops 3971520 | bytes 18004228 | tf_op jit(solution)/shard_map/reduce_sum | solution.py:171
  494.2 0.9 fusion.17
  (107 shorter events, 10.8 us)
Async XLA Ops:
  7.2 12.1 %copy-start = (s32[1,272]{1,0:T(1,128)S(1)}, s32[1,272]{1,0:T(1,128)}, u32[]{:S(2)}) copy-start(s32[1,272]{1,0:T(1,128)} %param.9) | copy-start | bytes 3268
  7.2 42.0 %copy-start.6 = (bf16[1,544,1176]{2,1,0:T(8,128)(2,1)S(1)}, bf16[1,544,1176]{2,1,0:T(8,128)(2,1)}, u32[]{:S(2)}) copy-start(bf16[1,544,1176]{2,1,0:T(8,128)(2,1)} %param.7) | copy-start | bytes 3838468
  7.2 96.2 %all-gather.5.cloned.1.call-start = ((), (), s32[]{:S(2)}) async-start(), calls=%async_computation.3 | async-start | bytes 9748480 | tf_op jit(solution)/shard_map/all_gather | solution.py:124
  12.2 42.8 %all-to-all-start = ((bf16[16,2,1]{1,2,0:T(2,128)(2,1)}), bf16[16,2,1]{1,2,0:T(2,128)(2,1)S(1)}, u32[]{:S(2)}, u32[]{:S(2)}) async-start(bf16[16,2,1]{1,2,0:T(2,128)(2,1)} %all_to_all.12), calls=%async_computation | async-start | bytes 16384 | tf_op jit(solution)/shard_map/all_to_all | solution.py:113
  42.2 20.2 %copy-start.12 = (u32[256]{0:T(256)S(1)}, u32[256]{0:T(256)}, u32[]{:S(2)}) copy-start(u32[256]{0:T(256)} %constant.79) | copy-start | bytes 3076
  42.2 21.5 %copy-start.11 = (bf16[224]{0:T(256)(128)(2,1)S(1)}, bf16[224]{0:T(256)(128)(2,1)}, u32[]{:S(2)}) copy-start(bf16[224]{0:T(256)(128)(2,1)} %param.11) | copy-start | bytes 1348
  55.0 43.9 %all-to-all-start.1 = ((bf16[32,32,1176]{2,1,0:T(8,128)(2,1)}), bf16[32,32,1176]{2,1,0:T(8,128)(2,1)}, u32[]{:S(2)}, u32[]{:S(2)}) async-start(bf16[32,32,1176]{2,1,0:T(8,128)(2,1)} %scatter_fusion), calls=%async_computation.1 | async-start | bytes 5242880 | tf_op jit(solution)/shard_map/all_to_all | solution.py:112
  62.3 296.0 %reduce-scatter.4.cloned.1.call-start = ((), (), s32[]{:S(2)}) async-start(), calls=%async_computation.5 | async-start | bytes 19496960 | tf_op jit(solution)/shard_map/reduce_scatter | solution.py:168
  111.4 24.2 %copy-start.2 = (f32[544,3584]{1,0:T(8,128)}, f32[544,3584]{1,0:T(8,128)S(1)}, u32[]{:S(2)}) copy-start(f32[544,3584]{1,0:T(8,128)S(1)} %get-tuple-element.69) | copy-start | bytes 23396356
  111.4 15.9 %copy-start.5 = (bf16[1,544,3584]{2,1,0:T(8,128)(2,1)S(1)}, bf16[1,544,3584]{2,1,0:T(8,128)(2,1)}, u32[]{:S(2)}) copy-start(bf16[1,544,3584]{2,1,0:T(8,128)(2,1)} %param.13) | copy-start | bytes 11698180
  111.5 15.9 %copy-start.7 = (f32[17,3584]{1,0:T(8,128)S(1)}, f32[17,3584]{1,0:T(8,128)}, u32[]{:S(2)}) copy-start(f32[17,3584]{1,0:T(8,128)} %get-tuple-element.57) | copy-start | bytes 731140
  111.5 15.9 %copy-start.8 = (f32[17,3584]{1,0:T(8,128)S(1)}, f32[17,3584]{1,0:T(8,128)}, u32[]{:S(2)}) copy-start(f32[17,3584]{1,0:T(8,128)} %get-tuple-element.55) | copy-start | bytes 731140
  111.5 15.9 %copy-start.9 = (f32[17,3584]{1,0:T(8,128)S(1)}, f32[17,3584]{1,0:T(8,128)}, u32[]{:S(2)}) copy-start(f32[17,3584]{1,0:T(8,128)} %get-tuple-element.53) | copy-start | bytes 731140
  111.5 15.9 %copy-start.10 = (f32[17,3584]{1,0:T(8,128)S(1)}, f32[17,3584]{1,0:T(8,128)}, u32[]{:S(2)}) copy-start(f32[17,3584]{1,0:T(8,128)} %get-tuple-element.51) | copy-start | bytes 731140
  112.8 22.9 %copy-start.4 = (bf16[544,3584]{1,0:T(8,128)(2,1)}, bf16[544,3584]{1,0:T(8,128)(2,1)S(1)}, u32[]{:S(2)}) copy-start(bf16[544,3584]{1,0:T(8,128)(2,1)S(1)} %multiply_convert_fusion) | copy-start | bytes 11698180
  112.9 13.1 %collective-permute-start.1 = (bf16[64,3584]{1,0:T(8,128)(2,1)S(1)}, bf16[64,3584]{1,0:T(8,128)(2,1)S(1)}, u32[]{:S(2)}, u32[]{:S(2)}) collective-permute-start(bf16[64,3584]{1,0:T(8,128)(2,1)S(1)} %get-tuple-element.47), channel_id=1, source_target_pairs={{16,0},{32,16},{48,32},{64,48},{80,64},{96,80},{112,96},{128,112},... | collective-permute-start | bytes 1376264 | tf_op jit(solution)/shard_map/ppermute | solution.py:20
  114.5 12.9 %collective-permute-start = (bf16[64,3584]{1,0:T(8,128)(2,1)S(1)}, bf16[64,3584]{1,0:T(8,128)(2,1)S(1)}, u32[]{:S(2)}, u32[]{:S(2)}) collective-permute-start(bf16[64,3584]{1,0:T(8,128)(2,1)S(1)} %get-tuple-element.46), channel_id=1, source_target_pairs={{0,16},{16,32},{32,48},{48,64},{64,80},{80,96},{96,112},{112,128},... | collective-permute-start | bytes 1376264 | tf_op jit(solution)/shard_map/ppermute | solution.py:18
  135.7 1.9 copy-start.3
  138.4 44.6 %collective-permute-start.3 = (bf16[64,3584]{1,0:T(8,128)(2,1)}, bf16[64,3584]{1,0:T(8,128)(2,1)}, u32[]{:S(2)}, u32[]{:S(2)}) collective-permute-start(bf16[64,3584]{1,0:T(8,128)(2,1)} %get-tuple-element.45), channel_id=1, source_target_pairs={{0,16},{16,32},{32,48},{48,64},{64,80},{80,96},{96,112},{112,128},... | collective-permute-start | bytes 1376264 | tf_op jit(solution)/shard_map/ppermute | solution.py:18
  143.9 39.1 %collective-permute-start.2 = (bf16[64,3584]{1,0:T(8,128)(2,1)S(1)}, bf16[64,3584]{1,0:T(8,128)(2,1)}, u32[]{:S(2)}, u32[]{:S(2)}) collective-permute-start(bf16[64,3584]{1,0:T(8,128)(2,1)S(1)} %get-tuple-element.44), channel_id=1, source_target_pairs={{16,0},{32,16},{48,32},{64,48},{80,64},{96,80},{112,96},{128,112},... | collective-permute-start | bytes 1376264 | tf_op jit(solution)/shard_map/ppermute | solution.py:20
  182.8 10.4 %slice-start = ((s8[7798784]{0:T(1024)(128)(4,1)}), s8[4194304]{0:T(1024)(128)(4,1)S(1)}, s32[]{:S(2)}) async-start(s8[7798784]{0:T(1024)(128)(4,1)} %bitcast.114), calls=%async_computation.6 | async-start | bytes 8388608
  183.0 10.3 %slice-start.1 = ((s8[7798784]{0:T(1024)(128)(4,1)}), s8[3604480]{0:T(1024)(128)(4,1)S(1)}, s32[]{:S(2)}) async-start(s8[7798784]{0:T(1024)(128)(4,1)} %bitcast.114), calls=%async_computation.7 | async-start | bytes 7208960
  248.4 238.4 %all-gather.7.cloned.1.call-start = ((), (), s32[]{:S(2)}) async-start(), calls=%async_computation.4 | async-start | bytes 19496960 | tf_op jit(solution)/shard_map/all_gather | solution.py:171
  486.8 9.2 %copy-start.1 = (s32[1,272]{1,0:T(1,128)S(1)}, s32[1,272]{1,0:T(1,128)}, u32[]{:S(2)}) copy-start(s32[1,272]{1,0:T(1,128)} %param.9) | copy-start | bytes 3268
Sparse Core Ops, SparseCore 0:
  9.9 60.7 all-gather.4
  248.5 109.7 reduce-scatter.3
  360.8 125.9 all-gather.6
